TPU v7x, 32 devices: a whole 2x2x4 slice. The times are simulated.
32 devices in a mesh: grp: 2 (over core), dev: 16 (over z, y, x).
Axes of the slice: x: 2, y: 2, z: 4, core: 2. Of those that a mesh axis runs over, the one named last changes fastest.
Arguments:
- embeds_t: bfloat16 [1024, 131072], P(None, ('grp', 'dev'))
- shard_counts: int32 [32], P(('grp', 'dev')), may hold values from 512 to 4096, as said below
- assignments: int32 [64, 131072], P('dev', 'grp'), may hold values from 0 to 255
Outputs:
- whitened: bfloat16 [1024, 131072], P('dev', 'grp')
- factor: float32 [1024, 1024], replicated
- centroids: float32 [64, 16, 256], P('dev')
Inputs may be any that keep to these rules, and one draw needn't show every extreme that they name: `shard_counts`: each shard holds between 512 and 4096 rows in its leading slots; one shard is full and one holds exactly 512.
All inputs are finite; a program needn't handle non-finite values.
Results may differ from a plain program's by a relative error of at most 0.0029.
Values may be sent and summed in bfloat16 or wider, within the bound.
A program may use at most 192 MiB of HBM per device.

v0:
```python
import jax
import jax.numpy as jnp
from jax import lax
from jax.sharding import PartitionSpec as P

CENT = 256


def body(embeds_t, shard_counts, assignments):
    row_dev = embeds_t.shape[1]
    counts_all = lax.all_gather(shard_counts, ("grp", "dev"), axis=0, tiled=True)
    slot_ids = jnp.arange(row_dev, dtype=jnp.int32)
    valid_slots = (slot_ids < shard_counts[0]).astype(jnp.float32)
    total_rows = jnp.sum(counts_all).astype(jnp.float32)
    as_float = embeds_t.astype(jnp.float32)
    col_sum = lax.psum(jnp.sum(as_float * valid_slots[None, :], axis=1), ("grp", "dev"))
    col_mean = col_sum / total_rows
    centred = (as_float - col_mean[:, None]) * valid_slots[None, :]
    gram_part = lax.dot_general(
        centred,
        centred,
        (((1,), (1,)), ((), ())),
        precision=lax.Precision.HIGHEST,
        preferred_element_type=jnp.float32,
    )
    gram_sum = lax.psum(gram_part, ("grp", "dev"))
    factor = jnp.linalg.cholesky(gram_sum / (total_rows - 1.0))
    white_local = lax.linalg.triangular_solve(factor, centred, left_side=True, lower=True).astype(
        jnp.bfloat16
    )
    owned_rows = lax.all_to_all(white_local, "dev", split_axis=0, concat_axis=1, tiled=True)
    sub_dev = assignments.shape[0]
    sub_width = owned_rows.shape[0] // sub_dev
    group_rows = owned_rows.shape[1]
    num_dev = lax.axis_size("dev")
    limits = lax.dynamic_slice_in_dim(counts_all, lax.axis_index("grp") * num_dev, num_dev)
    valid_rows = (slot_ids[None, :] < limits[:, None]).reshape(-1)
    blk_rows = min(4096, group_rows)
    centre_ids = jnp.arange(CENT, dtype=jnp.int32)

    def add_block(blk_index, carry):
        cent_sums, cent_counts = carry
        row_start = blk_index * blk_rows
        sub_rows = lax.dynamic_slice_in_dim(owned_rows, row_start, blk_rows, 1).reshape(
            sub_dev, sub_width, blk_rows
        )
        sub_assign = lax.dynamic_slice_in_dim(assignments, row_start, blk_rows, 1)
        row_ok = lax.dynamic_slice_in_dim(valid_rows, row_start, blk_rows, 0)
        one_hot = (
            (sub_assign[:, :, None] == centre_ids[None, None, :]) & row_ok[None, :, None]
        ).astype(jnp.bfloat16)
        cent_sums = cent_sums + jnp.einsum(
            "swb,sbc->swc", sub_rows, one_hot, preferred_element_type=jnp.float32
        )
        cent_counts = cent_counts + jnp.sum(one_hot, axis=1, dtype=jnp.float32)
        return (cent_sums, cent_counts)

    start_sums = jnp.zeros((sub_dev, sub_width, CENT), jnp.float32)
    start_counts = jnp.zeros((sub_dev, CENT), jnp.float32)
    cent_sums, cent_counts = lax.fori_loop(
        0, group_rows // blk_rows, add_block, (start_sums, start_counts)
    )
    cent_sums, cent_counts = lax.psum((cent_sums, cent_counts), "grp")
    centroids = cent_sums / (cent_counts[:, None, :] + 1.0)
    return (owned_rows, factor, centroids)


def solution(mesh):
    return jax.shard_map(
        body,
        mesh=mesh,
        in_specs=(P(None, ("grp", "dev")), P(("grp", "dev")), P("dev", "grp")),
        out_specs=(P("dev", "grp"), P(), P("dev", None, None)),
        check_vma=False,
    )
```

profile of v0, /device:TPU:0, one launch (start us, length us, event | category | flops | bytes accessed | tf_op | source)
XLA Modules:
  0.0 1166.8 jit_solution(4400866553339165679)
XLA Ops:
  8.0 41.9 %all-reduce.1 = s32[32]{0:T(128)S(1)} all-reduce(s32[32]{0:T(128)S(1)} %dynamic-update-slice.47), channel_id=1, replica_groups=mesh['grp'=2,'dev'=16] {'grp','dev'}, use_global_device_ids=true, to_apply=%add.1 | all-reduce | flops 32 | bytes 256
  56.3 40.1 %psum.28 = f32[1024]{0:T(1024)S(1)} all-reduce(f32[1024]{0:T(1024)S(1)} %fusion.11), channel_id=1, replica_groups=mesh['grp'=2,'dev'=16] {'grp','dev'}, use_global_device_ids=true, to_apply=%region_1.0 | all-reduce | flops 1024 | bytes 8192 | tf_op jit(solution)/shard_map/psum | solution.py:16
  96.4 63.0 %fusion.86 = f32[1024,1024]{0,1:T(8,128)} fusion(bf16[1024,4096]{1,0:T(8,128)(2,1)} %param.5, f32[1024]{0:T(1024)S(1)} %broadcast_divide_fusion.2, f32[4096]{0:T(1024)S(1)} %fusion.82), kind=kOutput, calls=%fused_computation.182 | convolution fusion | flops 51552190464 | bytes 12603392 | tf_op jit(solution)/shard_map/dot_general | solution.py:19
  159.5 12.1 %fusion.12 = f32[1024,4096]{1,0:T(8,128)} fusion(bf16[1024,4096]{1,0:T(8,128)(2,1)} %param.5, f32[1024]{0:T(1024)S(1)} %broadcast_divide_fusion.2, f32[4096]{0:T(1024)S(1)} %fusion.82), kind=kLoop, calls=%fused_computation.17 | loop fusion | flops 12582912 | bytes 25186304 | tf_op jit(solution)/shard_map/mul | solution.py:18
  171.7 130.9 %all-reduce.5.cloned.1.call-done = f32[1024,1024]{0,1:T(8,128)} async-done(((f32[1024,1024]{0,1:T(8,128)}), f32[1024,1024]{0,1:T(8,128)}) %all-reduce.5.cloned.1.call-update) | async-done | bytes 4194320 | tf_op jit(solution)/shard_map/psum | solution.py:26
  319.9 11.7 %cholesky.223 = f32[128,128]{1,0:T(8,128)S(1)} custom-call(f32[128,128]{1,0:T(8,128)S(1)} %cholesky.580), custom_call_target="Cholesky" | custom-call | tf_op jit(solution)/shard_map/jit(cholesky)/cholesky | solution.py:27
  331.6 9.8 custom-call.62
  347.9 11.9 %cholesky.244 = f32[128,128]{1,0:T(8,128)S(1)} custom-call(f32[128,128]{1,0:T(8,128)S(1)} %cholesky.584), custom_call_target="Cholesky" | custom-call | tf_op jit(solution)/shard_map/jit(cholesky)/cholesky | solution.py:27
  360.4 9.8 custom-call.63
  373.5 11.7 %cholesky.468 = f32[128,128]{1,0:T(8,128)S(1)} custom-call(f32[128,128]{1,0:T(8,128)S(1)} %cholesky.589), custom_call_target="Cholesky" | custom-call | tf_op jit(solution)/shard_map/jit(cholesky)/cholesky | solution.py:27
  386.5 9.8 custom-call.64
  399.8 11.9 %cholesky.487 = f32[128,128]{1,0:T(8,128)S(1)} custom-call(f32[128,128]{1,0:T(8,128)S(1)} %cholesky.594), custom_call_target="Cholesky" | custom-call | tf_op jit(solution)/shard_map/jit(cholesky)/cholesky | solution.py:27
  413.1 9.8 custom-call.65
  426.3 11.7 %cholesky.506 = f32[128,128]{1,0:T(8,128)S(1)} custom-call(f32[128,128]{1,0:T(8,128)S(1)} %cholesky.599), custom_call_target="Cholesky" | custom-call | tf_op jit(solution)/shard_map/jit(cholesky)/cholesky | solution.py:27
  439.3 10.2 custom-call.66
  452.8 11.7 %cholesky.526 = f32[128,128]{1,0:T(8,128)S(1)} custom-call(f32[128,128]{1,0:T(8,128)S(1)} %cholesky.604), custom_call_target="Cholesky" | custom-call | tf_op jit(solution)/shard_map/jit(cholesky)/cholesky | solution.py:27
  465.8 9.8 custom-call.67
  478.7 11.9 %cholesky.546 = f32[128,128]{1,0:T(8,128)S(1)} custom-call(f32[128,128]{1,0:T(8,128)S(1)} %cholesky.609), custom_call_target="Cholesky" | custom-call | tf_op jit(solution)/shard_map/jit(cholesky)/cholesky | solution.py:27
  491.9 9.8 custom-call.68
  504.4 11.7 %cholesky.564 = f32[128,128]{1,0:T(8,128)S(1)} custom-call(f32[128,128]{1,0:T(8,128)S(1)} %convolution_subtract_fusion.11), custom_call_target="Cholesky" | custom-call | tf_op jit(solution)/shard_map/jit(cholesky)/cholesky | solution.py:27
  529.9 22.5 %while.17 = (s32[]{:T(128)}, f32[1024,1024]{1,0:T(8,128)}, s32[8,2]{0,1:T(2,128)S(1)}, f32[8,128,128]{2,1,0:T(8,128)S(1)}, s32[]{:T(128)}) while((s32[]{:T(128)}, f32[1024,1024]{1,0:T(8,128)}, s32[8,2]{0,1:T(2,128)S(1)}, f32[8,128,128]{2,1,0:T(8,128)S(1)}, s32[]{:T(128)}) %tuple.85), condition=%wide.while_cond, body=%wide.while_body.sunk | while | flops 2 | bytes 131181 | solution.py:28
  552.4 78.8 %custom-call.69 = f32[8,128,128]{1,2,0:T(8,128)S(1)} custom-call(f32[8,128,128]{2,1,0:T(8,128)S(1)} %get-tuple-element.137), custom_call_target="InvertDiagBlocksLowerTriangular" | custom-call | tf_op jit(solution)/shard_map/triangular_solve | solution.py:28
  685.2 9.1 convolution_subtract_fusion.1
  700.5 9.8 convolution_subtract_fusion
  715.6 11.8 %convolution_subtract_fusion.4 = f32[128,4096]{1,0:T(8,128)S(1)} fusion(f32[896,4096]{1,0:T(8,128)} %constant_dynamic-update-slice_fusion.11, f32[1024,4096]{1,0:T(8,128)S(1)} %bitcast.117, f32[1024,1024]{1,0:T(8,128)} %get-tuple-element.357), kind=kOutput, calls=%fused_computation.36 | convolution fusion | flops 5637668864 | bytes 19333120 | tf_op jit(solution)/shard_map/triangular_solve | solution.py:28
  736.4 152.4 %all-to-all-done = bf16[16,64,4096]{2,1,0:T(8,128)(2,1)} async-done(((bf16[16,64,4096]{2,1,0:T(8,128)(2,1)}), bf16[16,64,4096]{2,1,0:T(8,128)(2,1)}, u32[]{:S(2)}, u32[]{:S(2)}) %all-to-all-start) | async-done | bytes 8388640 | tf_op jit(solution)/shard_map/all_to_all | solution.py:31
  888.8 7.9 copy.10
  896.7 208.9 %while.18 = (s32[]{:T(128)}, f32[4,16,256]{2,1,0:T(8,128)S(1)}, f32[4,256]{1,0:T(4,128)S(1)}, bf16[64,65536]{1,0:T(8,128)(2,1)}, s32[4,65536]{1,0:T(4,128)}, /*i...) while((s32[]{:T(128)}, f32[4,16,256]{2,1,0:T(8,128)S(1)}, ...), condition=%wide.region_22.23_spmd.clone, body=%wide.region_20.22_spmd.clone.sunk | while | flops 163611648 | bytes 1999018 | solution.py:60
  937.8 6.7 fusion.113
  963.9 6.7 fusion.113
  1029.2 6.7 fusion.113
  1108.1 50.1 %all-reduce.7.cloned.1.call-done = f32[4,16,256]{2,1,0:T(8,128)} async-done(((f32[4,16,256]{2,1,0:T(8,128)}), f32[4,16,256]{2,1,0:T(8,128)}) %all-reduce.7.cloned.1.call-update) | async-done | bytes 65552 | tf_op jit(solution)/shard_map/psum | solution.py:63
  (214 shorter events, 353.4 us)
Async XLA Ops:
  7.2 295.4 %all-reduce.5.cloned.1.call-start = ((), (), s32[]{:S(2)}) async-start(), calls=%async_computation.1 | async-start | bytes 8388608 | tf_op jit(solution)/shard_map/psum | solution.py:26
  317.9 2.0 copy-start
  631.3 27.0 %copy-start.1 = (f32[8,128,128]{1,2,0:T(8,128)}, f32[8,128,128]{1,2,0:T(8,128)S(1)}, u32[]{:S(2)}) copy-start(f32[8,128,128]{1,2,0:T(8,128)S(1)} %custom-call.69) | copy-start | bytes 1572868
  635.9 17.1 %slice-start = ((s8[16777216]{0:T(1024)(128)(4,1)}), s8[4194304]{0:T(1024)(128)(4,1)S(1)}, s32[]{:S(2)}) async-start(s8[16777216]{0:T(1024)(128)(4,1)} %bitcast.116), calls=%async_computation.3 | async-start | bytes 8388608
  639.3 13.7 %slice-start.1 = ((s8[16777216]{0:T(1024)(128)(4,1)}), s8[4194304]{0:T(1024)(128)(4,1)S(1)}, s32[]{:S(2)}) async-start(s8[16777216]{0:T(1024)(128)(4,1)} %bitcast.116), calls=%async_computation.4 | async-start | bytes 8388608
  643.0 10.0 slice-start.2
  645.9 7.1 slice-start.3
  731.1 157.6 %all-to-all-start = ((bf16[16,64,4096]{2,1,0:T(8,128)(2,1)}), bf16[16,64,4096]{2,1,0:T(8,128)(2,1)}, u32[]{:S(2)}, u32[]{:S(2)}) async-start(bf16[16,64,4096]{2,1,0:T(8,128)(2,1)} %bitcast.24), calls=%async_computation | async-start | bytes 16777216 | tf_op jit(solution)/shard_map/all_to_all | solution.py:31
  736.1 422.2 %all-reduce.7.cloned.1.call-start = ((), (), s32[]{:S(2)}) async-start(), calls=%async_computation.2 | async-start | bytes 131072 | tf_op jit(solution)/shard_map/psum | solution.py:63
  1105.6 2.5 copy-start.2
Sparse Core Ops, SparseCore 0:
  159.6 142.9 all-reduce.4
  1108.2 49.9 all-reduce.6
where the time goes:
time: 1180 us; the launch traced here: 1170 us
  other arithmetic  356 us (30%)
  waiting for transfers between devices  333 us (28%)
  matrix products  272 us (23%)
  local copies, waits for them, and re-layouts  92.9 us (8%)
  blocking collectives  84.6 us (7%)
  between operations  21 us (2%)
    another operation x30, other arithmetic, body(): factor = jnp.linalg.cholesky(gram_sum / (total_rows - 1.0))  172 us
    all_to_all x1, waiting for transfers between devices, body(): lax.all_to_all(white_local, 'dev', split_axis=0, concat_axis=1, tiled=True)  152 us
    psum x1, waiting for transfers between devices, body(): gram_sum = lax.psum(gram_part, ('grp', 'dev'))  131 us
    dot_general x16, matrix products, add_block(): jnp.einsum('swb,sbc->swc', sub_rows, one_hot, preferred_element_type=jnp....  108 us
    another operation x3, other arithmetic, body(): lax.linalg.triangular_solve(factor, centred, left_side=True, lower=True)  85.5 us
    another operation x15, matrix products, body(): lax.linalg.triangular_solve(factor, centred, left_side=True, lower=True)  78.5 us
    reduce_sum x16, other arithmetic, add_block(): cent_counts = cent_counts + jnp.sum(one_hot, axis=1, dtype=jnp.float32)  69.4 us
    dot_general x1, matrix products, body(): lax.dot_general(centred, centred, (((1,), (1,)), ((), ())), precision=lax...  63 us
  transfers between devices with their start and end apart: 3, of which 3 were waited for; matrix products, arithmetic and copies ran while one was open for 1% of the time, Pallas kernels for 0%

commit v1 on v0

--- a/solution.py
+++ b/solution.py
@@ -23,7 +23,7 @@
         precision=lax.Precision.HIGHEST,
         preferred_element_type=jnp.float32,
     )
-    gram_sum = lax.psum(gram_part, ("grp", "dev"))
+    gram_sum = lax.psum(lax.psum(gram_part, "dev"), "grp")
     factor = jnp.linalg.cholesky(gram_sum / (total_rows - 1.0))
     white_local = lax.linalg.triangular_solve(factor, centred, left_side=True, lower=True).astype(
         jnp.bfloat16

time: 1180 us -> 1240 us (1.051)
  waiting for transfers between devices: 333 us -> 394 us
    psum x1 -> x2, waiting for transfers between devices: 131 us -> 185 us  [body(): gram_sum = lax.psum(lax.psum(gram_part, 'dev'), 'grp')]
  transfers between devices with their start and end apart: 3 -> 4, of which waited for: 3 -> 4; matrix products, arithmetic and copies ran while one was open for 1% -> 1% of each run, Pallas kernels for 0% -> 0%
where the time goes in v1:
time: 1240 us; the launch traced here: 1230 us
  waiting for transfers between devices  394 us (32%)
  other arithmetic  358 us (29%)
  matrix products  272 us (22%)
  local copies, waits for them, and re-layouts  92.9 us (7%)
  blocking collectives  84.5 us (7%)
  between operations  20.7 us (2%)
    psum x2, waiting for transfers between devices, body(): gram_sum = lax.psum(lax.psum(gram_part, 'dev'), 'grp')  185 us
    another operation x30, other arithmetic, body(): factor = jnp.linalg.cholesky(gram_sum / (total_rows - 1.0))  172 us
    all_to_all x1, waiting for transfers between devices, body(): lax.all_to_all(white_local, 'dev', split_axis=0, concat_axis=1, tiled=True)  159 us
    dot_general x16, matrix products, add_block(): jnp.einsum('swb,sbc->swc', sub_rows, one_hot, preferred_element_type=jnp....  108 us
    another operation x3, other arithmetic, body(): lax.linalg.triangular_solve(factor, centred, left_side=True, lower=True)  85.5 us
    another operation x15, matrix products, body(): lax.linalg.triangular_solve(factor, centred, left_side=True, lower=True)  78.5 us
    reduce_sum x16, other arithmetic, add_block(): cent_counts = cent_counts + jnp.sum(one_hot, axis=1, dtype=jnp.float32)  69.4 us
    dot_general x1, matrix products, body(): lax.dot_general(centred, centred, (((1,), (1,)), ((), ())), precision=lax...  63 us
  transfers between devices with their start and end apart: 4, of which 4 were waited for; matrix products, arithmetic and copies ran while one was open for 1% of the time, Pallas kernels for 0%

profile of v1, /device:TPU:0, one launch (start us, length us, event | category | flops | bytes accessed | tf_op | source)
XLA Modules:
  0.0 1230.2 jit_solution(2512784921018566874)
XLA Ops:
  8.0 41.9 %all-reduce.1 = s32[32]{0:T(128)S(1)} all-reduce(s32[32]{0:T(128)S(1)} %dynamic-update-slice.47), channel_id=1, replica_groups=mesh['grp'=2,'dev'=16] {'grp','dev'}, use_global_device_ids=true, to_apply=%add.1 | all-reduce | flops 32 | bytes 256
  56.3 40.1 %psum.35 = f32[1024]{0:T(1024)S(1)} all-reduce(f32[1024]{0:T(1024)S(1)} %fusion.11), channel_id=1, replica_groups=mesh['grp'=2,'dev'=16] {'grp','dev'}, use_global_device_ids=true, to_apply=%region_1.0 | all-reduce | flops 1024 | bytes 8192 | tf_op jit(solution)/shard_map/psum | solution.py:16
  96.4 63.0 %fusion.86 = f32[1024,1024]{0,1:T(8,128)} fusion(bf16[1024,4096]{1,0:T(8,128)(2,1)} %param.5, f32[1024]{0:T(1024)S(1)} %broadcast_divide_fusion.2, f32[4096]{0:T(1024)S(1)} %fusion.82), kind=kOutput, calls=%fused_computation.182 | convolution fusion | flops 51552190464 | bytes 12603392 | tf_op jit(solution)/shard_map/dot_general | solution.py:19
  159.5 169.0 %all-reduce.6.cloned.1.call-done = f32[1024,1024]{0,1:T(8,128)} async-done(((f32[1024,1024]{0,1:T(8,128)}), f32[1024,1024]{0,1:T(8,128)}) %all-reduce.6.cloned.1.call-update) | async-done | bytes 4194320 | tf_op jit(solution)/shard_map/psum | solution.py:26
  328.6 14.0 %fusion.12 = f32[1024,4096]{1,0:T(8,128)} fusion(bf16[1024,4096]{1,0:T(8,128)(2,1)} %param.5, f32[1024]{0:T(1024)S(1)} %broadcast_divide_fusion.2, f32[4096]{0:T(1024)S(1)} %fusion.82), kind=kLoop, calls=%fused_computation.17 | loop fusion | flops 12582912 | bytes 25186304 | tf_op jit(solution)/shard_map/mul | solution.py:18
  342.6 15.6 %all-reduce.8.cloned.1.call-done = f32[1024,1024]{0,1:T(8,128)} async-done(((f32[1024,1024]{0,1:T(8,128)}), f32[1024,1024]{0,1:T(8,128)}) %all-reduce.8.cloned.1.call-update) | async-done | bytes 4194320 | tf_op jit(solution)/shard_map/psum | solution.py:26
  375.5 11.7 cholesky.223
  387.3 9.8 custom-call.62
  403.5 11.9 cholesky.244
  416.0 9.8 custom-call.63
  429.2 11.7 cholesky.468
  442.1 9.8 custom-call.64
  455.4 11.9 cholesky.487
  468.7 9.8 custom-call.65
  481.9 11.7 cholesky.506
  495.0 10.2 custom-call.66
  508.4 11.7 cholesky.526
  521.4 9.8 custom-call.67
  534.3 11.9 cholesky.546
  547.4 9.8 custom-call.68
  559.9 11.7 cholesky.564
  585.4 22.5 %while.17 = (s32[]{:T(128)}, f32[1024,1024]{1,0:T(8,128)}, s32[8,2]{0,1:T(2,128)S(1)}, f32[8,128,128]{2,1,0:T(8,128)S(1)}, s32[]{:T(128)}) while((s32[]{:T(128)}, f32[1024,1024]{1,0:T(8,128)}, s32[8,2]{0,1:T(2,128)S(1)}, f32[8,128,128]{2,1,0:T(8,128)S(1)}, s32[]{:T(128)}) %tuple.85), condition=%wide.while_cond, body=%wide.while_body.sunk | while | flops 2 | bytes 131181 | solution.py:28
  607.9 78.8 %custom-call.69 = f32[8,128,128]{1,2,0:T(8,128)S(1)} custom-call(f32[8,128,128]{2,1,0:T(8,128)S(1)} %get-tuple-element.137), custom_call_target="InvertDiagBlocksLowerTriangular" | custom-call | tf_op jit(solution)/shard_map/triangular_solve | solution.py:28
  740.7 9.1 convolution_subtract_fusion.1
  756.0 9.8 convolution_subtract_fusion
  771.1 11.8 convolution_subtract_fusion.4
  786.6 6.8 all-to-all-start
  793.8 158.9 %all-to-all-done = bf16[16,64,4096]{2,1,0:T(8,128)(2,1)} async-done(((bf16[16,64,4096]{2,1,0:T(8,128)(2,1)}), bf16[16,64,4096]{2,1,0:T(8,128)(2,1)}, u32[]{:S(2)}, u32[]{:S(2)}) %all-to-all-start) | async-done | bytes 8388640 | tf_op jit(solution)/shard_map/all_to_all | solution.py:31
  952.7 7.9 copy.10
  960.6 208.9 %while.18 = (s32[]{:T(128)}, f32[4,16,256]{2,1,0:T(8,128)S(1)}, f32[4,256]{1,0:T(4,128)S(1)}, bf16[64,65536]{1,0:T(8,128)(2,1)}, s32[4,65536]{1,0:T(4,128)}, /*i...) while((s32[]{:T(128)}, f32[4,16,256]{2,1,0:T(8,128)S(1)}, ...), condition=%wide.region_23.24_spmd.clone, body=%wide.region_21.23_spmd.clone.sunk | while | flops 163611648 | bytes 1999018 | solution.py:60
  975.6 6.7 fusion.113
  1172.0 50.0 %all-reduce.10.cloned.1.call-done = f32[4,16,256]{2,1,0:T(8,128)} async-done(((f32[4,16,256]{2,1,0:T(8,128)}), f32[4,16,256]{2,1,0:T(8,128)}) %all-reduce.10.cloned.1.call-update) | async-done | bytes 65552 | tf_op jit(solution)/shard_map/psum | solution.py:63
  (217 shorter events, 361.8 us)
Async XLA Ops:
  7.2 321.4 %all-reduce.6.cloned.1.call-start = ((), (), s32[]{:S(2)}) async-start(), calls=%async_computation.1 | async-start | bytes 8388608 | tf_op jit(solution)/shard_map/psum | solution.py:26
  159.5 198.7 %all-reduce.8.cloned.1.call-start = ((), (), s32[]{:S(2)}) async-start(), calls=%async_computation.2 | async-start | bytes 8388608 | tf_op jit(solution)/shard_map/psum | solution.py:26
  373.5 2.0 copy-start
  686.7 27.0 %copy-start.1 = (f32[8,128,128]{1,2,0:T(8,128)}, f32[8,128,128]{1,2,0:T(8,128)S(1)}, u32[]{:S(2)}) copy-start(f32[8,128,128]{1,2,0:T(8,128)S(1)} %custom-call.69) | copy-start | bytes 1572868
  691.4 17.1 %slice-start = ((s8[16777216]{0:T(1024)(128)(4,1)}), s8[4194304]{0:T(1024)(128)(4,1)S(1)}, s32[]{:S(2)}) async-start(s8[16777216]{0:T(1024)(128)(4,1)} %bitcast.116), calls=%async_computation.4 | async-start | bytes 8388608
  694.8 13.7 %slice-start.1 = ((s8[16777216]{0:T(1024)(128)(4,1)}), s8[4194304]{0:T(1024)(128)(4,1)S(1)}, s32[]{:S(2)}) async-start(s8[16777216]{0:T(1024)(128)(4,1)} %bitcast.116), calls=%async_computation.5 | async-start | bytes 8388608
  698.4 10.0 slice-start.2
  701.3 7.1 slice-start.3
  786.6 166.1 %all-to-all-start = ((bf16[16,64,4096]{2,1,0:T(8,128)(2,1)}), bf16[16,64,4096]{2,1,0:T(8,128)(2,1)}, u32[]{:S(2)}, u32[]{:S(2)}) async-start(bf16[16,64,4096]{2,1,0:T(8,128)(2,1)} %bitcast.24), calls=%async_computation | async-start | bytes 16777216 | tf_op jit(solution)/shard_map/all_to_all | solution.py:31
  793.5 428.6 %all-reduce.10.cloned.1.call-start = ((), (), s32[]{:S(2)}) async-start(), calls=%async_computation.3 | async-start | bytes 131072 | tf_op jit(solution)/shard_map/psum | solution.py:63
  1169.5 2.5 copy-start.2
Sparse Core Ops, SparseCore 0:
  159.6 168.9 all-reduce.5
  331.0 27.1 all-reduce.7
  1172.1 49.8 all-reduce.9
